TPU v7x, 256 devices: a whole 4x4x8 slice. The times are simulated.
256 devices in a mesh: dp: 32 (over y, z), vocab: 8 (over x, core).
Axes of the slice: x: 4, y: 4, z: 8, core: 2. Of those that a mesh axis runs over, the one named last changes fastest.
Arguments:
- draft_logits: bfloat16 [4096, 128000], P('dp', 'vocab'), may hold values from -15 to 250
- hidden: bfloat16 [4096, 2304], P('dp'), may hold values from -40 to 40
- embed_cot: bfloat16 [4096, 2304], P('dp'), may hold values from -0.59765625 to 0.59765625
- draft_ids: int32 [4096], P('dp'), may hold values from 0 to 127999, as said below
- target_ids: int32 [4096, 32], P('dp'), may hold values from 0 to 128255
- target_logits: float32 [4096, 32], P('dp'), may hold values from -8 to 240
- vocab_map: int32 [128256], replicated, may hold values from 0 to 127999
- master: float32 [128000, 2304], P(('vocab', 'dp')), may hold values from -6 to 6
- row_moment: float32 [128000], P(('vocab', 'dp')), may hold values from 0.0001 to 0.5
- col_moment: float32 [2304], replicated, may hold values from 0.003 to 0.03
Outputs:
- direction: bfloat16 [128000, 2304], P(('vocab', 'dp'))
- row_new: float32 [128000], P(('vocab', 'dp'))
- col_new: float32 [2304], replicated
- next_rows: bfloat16 [4096, 2304], P('dp')
Inputs may be any that keep to these rules, and one draw needn't show every extreme that they name: `draft_ids`: among the 128 tokens of one index of dp, at most 20 have draft ids in any one block of 16000 consecutive ids, and some block holds exactly 20 of them.
All inputs are finite; a program needn't handle non-finite values.
Results may differ from a plain program's by a relative error of at most 0.0073.
Values may be sent and summed in bfloat16 or wider, within the bound.
No kernel may reach another device: no remote copies, remote signals or barrier semaphores. Data moves between devices by JAX's collectives and lax.ppermute only.
A program may use at most 128 MiB of HBM per device.

v0:
```python
import jax
import jax.numpy as jnp
from jax import lax
from jax.sharding import PartitionSpec as P

DECAY_RATE = 0.9
STEP_SCALE = 0.01
SQUARE_EPS = 1e-30


def body(
    draft_logits,
    hidden,
    embed_cot,
    draft_ids,
    target_ids,
    target_logits,
    vocab_map,
    master,
    row_moment,
    col_moment,
):
    tokens_here, shard_cols = draft_logits.shape
    owned_rows, features = master.shape
    dp_count = lax.axis_size("dp")
    vocab_count = lax.axis_size("vocab")
    vocab_index = lax.axis_index("vocab")
    dp_index = lax.axis_index("dp")
    logits = draft_logits.astype(jnp.float32)
    local_max = jnp.max(logits, axis=1)
    highest = lax.pmax(local_max, "vocab")
    totals = lax.psum(jnp.sum(jnp.exp(logits - highest[:, None]), axis=1), "vocab")
    probs = jnp.exp(logits - highest[:, None]) / totals[:, None]
    shifted = target_logits - jnp.max(target_logits, axis=1, keepdims=True)
    target_exp = jnp.exp(shifted)
    weights = target_exp / jnp.sum(target_exp, axis=1, keepdims=True)
    mapped = vocab_map[target_ids] - vocab_index * shard_cols
    inside = (mapped >= 0) & (mapped < shard_cols)
    token_index = jnp.broadcast_to(
        jnp.arange(tokens_here, dtype=jnp.int32)[:, None], target_ids.shape
    )
    target = (
        jnp.zeros((tokens_here, shard_cols), jnp.float32)
        .at[token_index, jnp.clip(mapped, 0, shard_cols - 1)]
        .add(jnp.where(inside, weights, jnp.zeros_like(weights)))
    )
    slopes = (probs - target).astype(jnp.bfloat16)
    owned_slopes = lax.all_to_all(slopes, "dp", split_axis=1, concat_axis=0, tiled=True)
    head_grad = jnp.einsum(
        "tv,td->vd",
        owned_slopes,
        lax.all_gather(hidden, "dp", axis=0, tiled=True),
        preferred_element_type=jnp.float32,
    )
    block_base = vocab_index * shard_cols
    in_shard = (draft_ids >= block_base) & (draft_ids < block_base + shard_cols)
    slot_count = tokens_here // vocab_count + tokens_here // (4 * vocab_count)
    position = jnp.cumsum(in_shard.astype(jnp.int32)) - 1
    placing = (position[None, :] == jnp.arange(slot_count, dtype=jnp.int32)[:, None]) & in_shard[
        None, :
    ]
    filled = jnp.any(placing, axis=1)
    packed_ids = jnp.where(filled, jnp.sum(jnp.where(placing, draft_ids[None, :], 0), axis=1), -1)
    placing_half = placing.astype(jnp.bfloat16)
    packed_cot = jnp.dot(placing_half, embed_cot, preferred_element_type=jnp.float32).astype(
        jnp.bfloat16
    )
    all_ids, all_cot = (
        lax.all_gather(packed_ids, "dp", axis=0, tiled=True),
        lax.all_gather(packed_cot, "dp", axis=0, tiled=True),
    )
    row_base = (vocab_index * dp_count + dp_index) * owned_rows
    row_iota = jnp.arange(owned_rows, dtype=jnp.int32)
    matches = (all_ids[None, :] - row_base == row_iota[:, None]).astype(jnp.bfloat16)
    grad = head_grad + jnp.dot(matches, all_cot, preferred_element_type=jnp.float32)
    squares = grad * grad + SQUARE_EPS
    row_new = DECAY_RATE * row_moment + (1.0 - DECAY_RATE) * jnp.mean(squares, axis=1)
    column_total, row_total = lax.psum(
        (jnp.sum(squares, axis=0), jnp.sum(row_new)), ("dp", "vocab")
    )
    vocab_rows = owned_rows * dp_count * vocab_count
    col_new = DECAY_RATE * col_moment + (1.0 - DECAY_RATE) * (column_total / vocab_rows)
    scale = row_new[:, None] * col_new[None, :] / (row_total / vocab_rows)
    direction = grad / jnp.sqrt(scale)
    fresh = (master - STEP_SCALE * direction).astype(jnp.bfloat16)
    wanted = all_ids - row_base
    select = (wanted[:, None] == row_iota[None, :]).astype(jnp.bfloat16)
    slot_values = lax.psum_scatter(
        jnp.dot(select, fresh, preferred_element_type=jnp.float32).astype(jnp.bfloat16),
        "dp",
        scatter_dimension=0,
        tiled=True,
    )
    spread = jnp.einsum("st,sd->td", placing_half, slot_values, preferred_element_type=jnp.float32)
    next_rows = lax.psum(spread.astype(jnp.bfloat16), "vocab")
    return (direction.astype(jnp.bfloat16), row_new, col_new, next_rows)


def solution(mesh):
    in_specs = (
        P("dp", "vocab"),
        P("dp", None),
        P("dp", None),
        P("dp"),
        P("dp", None),
        P("dp", None),
        P(),
        P(("vocab", "dp"), None),
        P(("vocab", "dp")),
        P(),
    )
    out_specs = (P(("vocab", "dp"), None), P(("vocab", "dp")), P(), P("dp", None))
    return jax.shard_map(body, mesh=mesh, in_specs=in_specs, out_specs=out_specs, check_vma=False)
```

profile of v0, /device:TPU:8, one launch (start us, length us, event | category | flops | bytes accessed | tf_op | source)
XLA Modules:
  0.0 619.0 jit_solution(5468428876925927025)
XLA Ops:
  11.0 23.0 %gather_fusion = s32[4096]{0:T(1024)S(1)} fusion(s32[128256]{0:T(1024)S(1)} %copy-done.2, s32[4096]{0:T(1024)S(1)} %broadcast_clamp_fusion), kind=kCustom, calls=%fused_computation | custom fusion | bytes 49152 | tf_op jit(solution)/shard_map/gather | solution.py:37
  35.2 31.6 %scatter_custom_fusion = f32[2048000]{0:T(1024)} fusion(s32[4096]{0:T(1024)S(1)} %reshape.100, f32[4096]{0:T(1024)S(1)} %reshape.102, f32[]{:T(128)} %constant.21.clone.1), kind=kCustom, calls=%fused_computation.10 | custom fusion | flops 4096 | bytes 8192004
  66.8 9.1 %reshape.90 = f32[128,16000]{1,0:T(8,128)} reshape(f32[2048000]{0:T(1024)} %scatter_custom_fusion) | data formatting | bytes 16384000 | tf_op jit(solution)/shard_map/scatter-add | solution.py:45
  75.9 2.9 reduce_max.23
  78.8 13.1 %pmax.7 = f32[128]{0:T(128)S(1)} all-reduce(bf16[128]{0:T(256)(128)(2,1)S(1)} %reduce_max.23), channel_id=1, replica_groups=mesh['dp'=32,'vocab'=8] {'vocab'}, use_global_device_ids=true, to_apply=%region_1.0 | all-reduce | flops 128 | bytes 768 | tf_op jit(solution)/shard_map/pmax | solution.py:31
  91.9 3.7 fusion.1
  95.5 12.4 %psum.28 = f32[128]{0:T(128)S(1)} all-reduce(f32[128]{0:T(128)S(1)} %fusion.1), channel_id=1, replica_groups=mesh['dp'=32,'vocab'=8] {'vocab'}, use_global_device_ids=true, to_apply=%region_3.0 | all-reduce | flops 128 | bytes 1024 | tf_op jit(solution)/shard_map/psum | solution.py:32
  108.0 6.9 %subtract_convert_fusion = bf16[128,16000]{1,0:T(8,128)(2,1)} fusion(f32[128,16000]{1,0:T(8,128)} %reshape.90, bf16[128,16000]{1,0:T(8,128)(2,1)} %param.10, f32[128]{0:T(128)S(1)} %psum.28, f32[128]{0:T(128)S(1)} %pmax.7), kind=kLoop, calls=%fused_computation.2 | loop fusion | flops 10240000 | bytes 16385024 | tf_op jit(solution)/shard_map/convert_element_type | solution.py:47
  114.9 10.9 %reshape.126 = bf16[128,32,500]{2,1,0:T(8,128)(2,1)} reshape(bf16[128,16000]{1,0:T(8,128)(2,1)} %subtract_convert_fusion) | data formatting | bytes 8192000 | tf_op jit(solution)/shard_map/all_to_all | solution.py:48
  125.7 7.9 %copy.40 = bf16[128,32,500]{0,2,1:T(8,128)(2,1)} copy(bf16[128,32,500]{2,1,0:T(8,128)(2,1)} %reshape.126) | data formatting | bytes 8192000 | tf_op jit(solution)/shard_map/all_to_all | solution.py:48
  133.6 11.5 %all-to-all-start = ((bf16[128,32,500]{0,2,1:T(8,128)(2,1)}), bf16[128,32,500]{0,2,1:T(8,128)(2,1)}, u32[]{:S(2)}, u32[]{:S(2)}) async-start(bf16[128,32,500]{0,2,1:T(8,128)(2,1)} %copy.40), calls=%async_computation | async-start | bytes 8257536 | tf_op jit(solution)/shard_map/all_to_all | solution.py:48
  146.8 146.2 %all-reduce = s32[640]{0:T(1024)S(1)} all-reduce(s32[640]{0:T(1024)S(1)} %select_dynamic-update-slice_fusion), channel_id=1, replica_groups=mesh['dp'=32,'vocab'=8] {'dp'}, use_global_device_ids=true, to_apply=%add | all-reduce | flops 640 | bytes 5120
  293.0 3.8 reshape.123
  296.8 4.1 fusion.8
  301.0 6.6 %copy.38 = bf16[32,128,500]{2,1,0:T(8,128)(2,1)} copy(bf16[32,128,500]{1,2,0:T(8,128)(2,1)} %bitcast) | data formatting | bytes 8192000 | tf_op jit(solution)/shard_map/all_to_all | solution.py:48
  307.5 18.4 %all-gather.4.cloned.1.call-done = bf16[4096,2304]{1,0:T(8,128)(2,1)} async-done(((bf16[128,2304]{1,0:T(8,128)(2,1)}), bf16[4096,2304]{1,0:T(8,128)(2,1)}) %all-gather.4.cloned.1.call-update) | async-done | bytes 18874384 | tf_op jit(solution)/shard_map/all_gather | solution.py:52
  326.0 18.5 %fusion.4 = (f32[2304]{0:T(1024)S(1)}, f32[500]{0:T(512)S(1)}, f32[500,2304]{1,0:T(8,128)}) fusion(f32[500,2304]{1,0:T(8,128)} %fusion.8, bf16[4096,500]{1,0:T(8,128)(2,1)} %bitcast.14, bf16[4096,2304]{1,0:T(8,128)(2,1)} %all-gather.4.cloned.1.call-done), kind=kOutput, calls=%fused_computation.12 | convolution fusion | flops 9442941952 | bytes 32197584 | tf_op jit(solution)/shard_map/tv,td->vd/dot_general | solution.py:49
  345.1 74.8 %all-reduce.3 = (f32[]{:T(128)}, f32[2304]{0:T(1024)S(1)}) all-reduce(f32[]{:T(128)} %get-tuple-element.8, f32[2304]{0:T(1024)S(1)} %get-tuple-element.4), channel_id=1, replica_groups=mesh['dp'=32,'vocab'=8] {'dp','vocab'}, use_global_device_ids=true, to_apply=%region_14.15 | all-reduce | flops 2305 | bytes 18440 | tf_op jit(solution)/shard_map/psum | solution.py:78
  420.6 5.8 convolution_convert_fusion
  426.4 79.6 %fusion = bf16[24,2304]{1,0:T(8,128)(2,1)S(1)} fusion(bf16[640,2304]{1,0:T(8,128)(2,1)S(1)} %convolution_convert_fusion), kind=kCustom, calls=%all-reduce-scatter | all-reduce-scatter fusion | flops 1769473 | bytes 3060736
  506.1 1.9 collective-permute-start.5
  508.0 2.1 collective-permute-start
  510.2 4.7 collective-permute-start.1
  514.9 3.3 collective-permute-start.2
  518.1 7.8 %collective-permute-start.3 = (bf16[24,2304]{1,0:T(8,128)(2,1)S(1)}, bf16[24,2304]{1,0:T(8,128)(2,1)S(1)}, u32[]{:S(2)}, u32[]{:S(2)}) collective-permute-start(bf16[24,2304]{1,0:T(8,128)(2,1)S(1)} %fusion), channel_id=1, source_target_pairs={{0,32},{8,40},{16,48},{24,56},{32,64},{40,72},{48,80},{56,88},{64,... | collective-permute-start | bytes 331784
  526.0 8.8 %collective-permute-start.4 = (bf16[24,2304]{1,0:T(8,128)(2,1)S(1)}, bf16[24,2304]{1,0:T(8,128)(2,1)S(1)}, u32[]{:S(2)}, u32[]{:S(2)}) collective-permute-start(bf16[24,2304]{1,0:T(8,128)(2,1)S(1)} %fusion), channel_id=1, source_target_pairs={{0,40},{8,48},{16,56},{24,64},{32,72},{40,80},{48,88},{56,96},{64,... | collective-permute-start | bytes 331784
  535.5 1.6 collective-permute-done.4
  537.1 2.1 concatenate.4
  539.2 1.9 convolution_convert_fusion.1
  541.1 4.5 fusion.23
  545.6 64.9 %all-reduce.6.cloned.1.call-done = bf16[128,2304]{1,0:T(8,128)(2,1)} async-done(((bf16[128,2304]{1,0:T(8,128)(2,1)}), bf16[128,2304]{1,0:T(8,128)(2,1)}) %all-reduce.6.cloned.1.call-update) | async-done | bytes 589840 | tf_op jit(solution)/shard_map/psum | solution.py:95
  610.5 1.9 copy.43
  (78 shorter events, 6.6 us)
Async XLA Ops:
  7.2 1.2 copy-start
  7.2 3.8 copy-start.2
  7.2 285.8 %all-gather.6.cloned.1.call-start = ((), (), s32[]{:S(2)}) async-start(), calls=%async_computation.3 | async-start | bytes 3649536 | tf_op jit(solution)/shard_map/all_gather | solution.py:70
  8.0 138.6 %copy-start.9 = (pred[128]{0:T(512)(128)(4,1)}, pred[128]{0:T(512)(128)(4,1)S(1)}, u32[]{:S(2)}) copy-start(pred[128]{0:T(512)(128)(4,1)S(1)} %get-tuple-element.11) | copy-start | bytes 388
  8.4 138.2 %copy-start.8 = (s32[128]{0:T(128)}, s32[128]{0:T(128)S(1)}, u32[]{:S(2)}) copy-start(s32[128]{0:T(128)S(1)} %add_reduce_fusion) | copy-start | bytes 1540
  9.3 316.7 %all-gather.4.cloned.1.call-start = ((), (), s32[]{:S(2)}) async-start(), calls=%async_computation.1 | async-start | bytes 19464192 | tf_op jit(solution)/shard_map/all_gather | solution.py:52
  11.0 23.3 %copy-start.14 = (s32[2]{0:T(128)S(1)}, s32[2]{0:T(128)}, u32[]{:S(2)}) copy-start(s32[2]{0:T(128)} %constant.64) | copy-start | bytes 28
  11.0 23.3 %copy-start.13 = (s32[2]{0:T(128)S(1)}, s32[2]{0:T(128)}, u32[]{:S(2)}) copy-start(s32[2]{0:T(128)} %constant.67) | copy-start | bytes 28
  11.0 23.7 %copy-start.4 = (f32[128,32]{0,1:T(8,128)S(1)}, f32[128,32]{0,1:T(8,128)}, u32[]{:S(2)}) copy-start(f32[128,32]{0,1:T(8,128)} %param.15) | copy-start | bytes 49156
  133.6 11.6 %copy-start.12 = (u32[256]{0:T(256)S(1)}, u32[256]{0:T(256)}, u32[]{:S(2)}) copy-start(u32[256]{0:T(256)} %constant.74) | copy-start | bytes 3076
  133.6 13.0 %copy-start.11 = (s32[128]{0:T(128)S(1)}, s32[128]{0:T(128)}, u32[]{:S(2)}) copy-start(s32[128]{0:T(128)} %param.13) | copy-start | bytes 1540
  133.6 167.3 %all-to-all-start = ((bf16[128,32,500]{0,2,1:T(8,128)(2,1)}), bf16[128,32,500]{0,2,1:T(8,128)(2,1)}, u32[]{:S(2)}, u32[]{:S(2)}) async-start(bf16[128,32,500]{0,2,1:T(8,128)(2,1)} %copy.40), calls=%async_computation | async-start | bytes 8257536 | tf_op jit(solution)/shard_map/all_to_all | solution.py:48
  145.2 465.4 %all-reduce.6.cloned.1.call-start = ((), (), s32[]{:S(2)}) async-start(), calls=%async_computation.2 | async-start | bytes 1179648 | tf_op jit(solution)/shard_map/psum | solution.py:95
  326.0 18.5 %copy-start.10 = (f32[500]{0:T(512)S(1)}, f32[500]{0:T(512)}, u32[]{:S(2)}) copy-start(f32[500]{0:T(512)} %param.18) | copy-start | bytes 6004
  326.0 94.0 %copy-start.6 = (f32[2304]{0:T(1024)S(1)}, f32[2304]{0:T(1024)}, u32[]{:S(2)}) copy-start(f32[2304]{0:T(1024)} %param.19) | copy-start | bytes 27652
  345.1 196.0 %copy-start.7 = (f32[500]{0:T(512)}, f32[500]{0:T(512)S(1)}, u32[]{:S(2)}) copy-start(f32[500]{0:T(512)S(1)} %get-tuple-element.16) | copy-start | bytes 6004
  420.0 121.1 %copy-start.5 = (f32[2304]{0:T(1024)}, f32[2304]{0:T(1024)S(1)}, u32[]{:S(2)}) copy-start(f32[2304]{0:T(1024)S(1)} %multiply_add_fusion.1) | copy-start | bytes 27652
  506.1 29.4 %copy-start.3 = (bf16[24,2304]{1,0:T(8,128)(2,1)}, bf16[24,2304]{1,0:T(8,128)(2,1)S(1)}, u32[]{:S(2)}) copy-start(bf16[24,2304]{1,0:T(8,128)(2,1)S(1)} %fusion) | copy-start | bytes 331780
  506.1 19.9 %collective-permute-start.5 = (bf16[4,2304]{1,0:T(4,128)(2,1)S(1)}, bf16[4,2304]{1,0:T(4,128)(2,1)S(1)}, u32[]{:S(2)}, u32[]{:S(2)}) collective-permute-start(bf16[4,2304]{1,0:T(4,128)(2,1)S(1)} %slice.2), channel_id=1, source_target_pairs={{0,48},{8,56},{16,64},{24,72},{32,80},{40,88},{48,96},{56,104},{64... | collective-permute-start | bytes 55304
  508.0 27.4 %collective-permute-start = (bf16[24,2304]{1,0:T(8,128)(2,1)S(1)}, bf16[24,2304]{1,0:T(8,128)(2,1)S(1)}, u32[]{:S(2)}, u32[]{:S(2)}) collective-permute-start(bf16[24,2304]{1,0:T(8,128)(2,1)S(1)} %fusion), channel_id=1, source_target_pairs={{0,8},{8,16},{16,24},{24,32},{32,40},{40,48},{48,56},{56,64},{64,7... | collective-permute-start | bytes 331784
  510.2 25.3 %collective-permute-start.1 = (bf16[24,2304]{1,0:T(8,128)(2,1)S(1)}, bf16[24,2304]{1,0:T(8,128)(2,1)S(1)}, u32[]{:S(2)}, u32[]{:S(2)}) collective-permute-start(bf16[24,2304]{1,0:T(8,128)(2,1)S(1)} %fusion), channel_id=1, source_target_pairs={{0,16},{8,24},{16,32},{24,40},{32,48},{40,56},{48,64},{56,72},{64,... | collective-permute-start | bytes 331784
  514.9 20.6 %collective-permute-start.2 = (bf16[24,2304]{1,0:T(8,128)(2,1)S(1)}, bf16[24,2304]{1,0:T(8,128)(2,1)S(1)}, u32[]{:S(2)}, u32[]{:S(2)}) collective-permute-start(bf16[24,2304]{1,0:T(8,128)(2,1)S(1)} %fusion), channel_id=1, source_target_pairs={{0,24},{8,32},{16,40},{24,48},{32,56},{40,64},{48,72},{56,80},{64,... | collective-permute-start | bytes 331784
  518.1 17.3 %collective-permute-start.3 = (bf16[24,2304]{1,0:T(8,128)(2,1)S(1)}, bf16[24,2304]{1,0:T(8,128)(2,1)S(1)}, u32[]{:S(2)}, u32[]{:S(2)}) collective-permute-start(bf16[24,2304]{1,0:T(8,128)(2,1)S(1)} %fusion), channel_id=1, source_target_pairs={{0,32},{8,40},{16,48},{24,56},{32,64},{40,72},{48,80},{56,88},{64,... | collective-permute-start | bytes 331784
  526.0 11.1 %collective-permute-start.4 = (bf16[24,2304]{1,0:T(8,128)(2,1)S(1)}, bf16[24,2304]{1,0:T(8,128)(2,1)S(1)}, u32[]{:S(2)}, u32[]{:S(2)}) collective-permute-start(bf16[24,2304]{1,0:T(8,128)(2,1)S(1)} %fusion), channel_id=1, source_target_pairs={{0,40},{8,48},{16,56},{24,64},{32,72},{40,80},{48,88},{56,96},{64,... | collective-permute-start | bytes 331784
  537.1 75.3 %copy-start.1 = (bf16[128,2304]{1,0:T(8,128)(2,1)S(1)}, bf16[128,2304]{1,0:T(8,128)(2,1)}, u32[]{:S(2)}) copy-start(bf16[128,2304]{1,0:T(8,128)(2,1)} %param.12) | copy-start | bytes 1769476
Sparse Core Ops, SparseCore 0:
  11.2 81.9 all-gather.5
  95.7 230.1 all-gather.3
  541.2 69.2 all-reduce.5
where the time goes:
time: 620 us; the launch traced here: 619 us
  blocking collectives  326 us (53%)
  waiting for transfers between devices  85.8 us (14%)
  local copies, waits for them, and re-layouts  66.8 us (11%)
  other arithmetic  52.7 us (8%)
  starting transfers between devices  40.2 us (6%)
  matrix products  31.2 us (5%)
  between operations  16.1 us (3%)
    unnamed x2, blocking collectives  226 us
    psum x1, blocking collectives, body(): lax.psum((jnp.sum(squares, axis=0), jnp.sum(row_new)), ('dp', 'vocab'))  74.8 us
    psum x1, waiting for transfers between devices, body(): next_rows = lax.psum(spread.astype(jnp.bfloat16), 'vocab')  64.9 us
    unnamed x5, other arithmetic  31.9 us
    unnamed x6, starting transfers between devices  28.6 us
    all_to_all x3, local copies, waits for them, and re-layouts, body(): lax.all_to_all(slopes, 'dp', split_axis=1, concat_axis=0, tiled=True)  25.3 us
    gather x1, local copies, waits for them, and re-layouts, body(): mapped = vocab_map[target_ids] - vocab_index * shard_cols  23 us
    dot_general x1, matrix products, body(): jnp.einsum('tv,td->vd', owned_slopes, lax.all_gather(hidden, 'dp', axis=0...  18.5 us
  transfers between devices with their start and end apart: 10, of which 4 were waited for; matrix products, arithmetic and copies ran while one was open for 19% of the time, Pallas kernels for 0%

commit v1 on v0

--- a/solution.py
+++ b/solution.py
@@ -76,7 +76,7 @@
     squares = grad * grad + SQUARE_EPS
     row_new = DECAY_RATE * row_moment + (1.0 - DECAY_RATE) * jnp.mean(squares, axis=1)
     column_total, row_total = lax.psum(
-        (jnp.sum(squares, axis=0), jnp.sum(row_new)), ("dp", "vocab")
+        lax.psum((jnp.sum(squares, axis=0), jnp.sum(row_new)), "dp"), "vocab"
     )
     vocab_rows = owned_rows * dp_count * vocab_count
     col_new = DECAY_RATE * col_moment + (1.0 - DECAY_RATE) * (column_total / vocab_rows)

time: 620 us -> 707 us (1.14)
  blocking collectives: 326 us -> 415 us
    psum x1 -> x2, blocking collectives: 74.8 us -> 154 us  [the longest x1 129 us: body(): lax.psum((jnp.sum(squares, axis=0), jnp.sum(row_new)), 'dp')]
    unnamed x2, blocking collectives: 226 us -> 235 us
  transfers between devices with their start and end apart: 10 -> 10, of which waited for: 4 -> 3; matrix products, arithmetic and copies ran while one was open for 19% -> 17% of each run, Pallas kernels for 0% -> 0%
where the time goes in v1:
time: 707 us; the launch traced here: 706 us
  blocking collectives  415 us (59%)
  waiting for transfers between devices  84.9 us (12%)
  local copies, waits for them, and re-layouts  66.8 us (9%)
  other arithmetic  52.7 us (7%)
  starting transfers between devices  39.4 us (6%)
  matrix products  31.2 us (4%)
  between operations  16.1 us (2%)
    unnamed x2, blocking collectives  235 us
    psum x1, blocking collectives, body(): lax.psum((jnp.sum(squares, axis=0), jnp.sum(row_new)), 'dp')  129 us
    psum x1, waiting for transfers between devices, body(): next_rows = lax.psum(spread.astype(jnp.bfloat16), 'vocab')  64.1 us
    unnamed x5, other arithmetic  31.9 us
    unnamed x6, starting transfers between devices  27.7 us
    all_to_all x3, local copies, waits for them, and re-layouts, body(): lax.all_to_all(slopes, 'dp', split_axis=1, concat_axis=0, tiled=True)  25.3 us
    psum x1, blocking collectives, body(): lax.psum(lax.psum((jnp.sum(squares, axis=0), jnp.sum(row_new)), 'dp'), 'v...  24.6 us
    gather x1, local copies, waits for them, and re-layouts, body(): mapped = vocab_map[target_ids] - vocab_index * shard_cols  23 us
  transfers between devices with their start and end apart: 10, of which 3 were waited for; matrix products, arithmetic and copies ran while one was open for 17% of the time, Pallas kernels for 0%

profile of v1, /device:TPU:8, one launch (start us, length us, event | category | flops | bytes accessed | tf_op | source)
XLA Modules:
  0.0 705.7 jit_solution(5819675606144294466)
XLA Ops:
  11.0 23.0 %gather_fusion = s32[4096]{0:T(1024)S(1)} fusion(s32[128256]{0:T(1024)S(1)} %copy-done.2, s32[4096]{0:T(1024)S(1)} %broadcast_clamp_fusion), kind=kCustom, calls=%fused_computation | custom fusion | bytes 49152 | tf_op jit(solution)/shard_map/gather | solution.py:37
  35.2 31.6 %scatter_custom_fusion = f32[2048000]{0:T(1024)} fusion(s32[4096]{0:T(1024)S(1)} %reshape.100, f32[4096]{0:T(1024)S(1)} %reshape.102, f32[]{:T(128)} %constant.21.clone.1), kind=kCustom, calls=%fused_computation.10 | custom fusion | flops 4096 | bytes 8192004
  66.8 9.1 %reshape.90 = f32[128,16000]{1,0:T(8,128)} reshape(f32[2048000]{0:T(1024)} %scatter_custom_fusion) | data formatting | bytes 16384000 | tf_op jit(solution)/shard_map/scatter-add | solution.py:45
  75.9 2.9 reduce_max.23
  78.8 13.1 %pmax.7 = f32[128]{0:T(128)S(1)} all-reduce(bf16[128]{0:T(256)(128)(2,1)S(1)} %reduce_max.23), channel_id=1, replica_groups=mesh['dp'=32,'vocab'=8] {'vocab'}, use_global_device_ids=true, to_apply=%region_1.0 | all-reduce | flops 128 | bytes 768 | tf_op jit(solution)/shard_map/pmax | solution.py:31
  91.9 3.7 fusion.1
  95.5 12.4 %psum.42 = f32[128]{0:T(128)S(1)} all-reduce(f32[128]{0:T(128)S(1)} %fusion.1), channel_id=1, replica_groups=mesh['dp'=32,'vocab'=8] {'vocab'}, use_global_device_ids=true, to_apply=%region_3.0 | all-reduce | flops 128 | bytes 1024 | tf_op jit(solution)/shard_map/psum | solution.py:32
  108.0 6.9 subtract_convert_fusion
  114.9 10.9 %reshape.126 = bf16[128,32,500]{2,1,0:T(8,128)(2,1)} reshape(bf16[128,16000]{1,0:T(8,128)(2,1)} %subtract_convert_fusion) | data formatting | bytes 8192000 | tf_op jit(solution)/shard_map/all_to_all | solution.py:48
  125.7 7.9 %copy.40 = bf16[128,32,500]{0,2,1:T(8,128)(2,1)} copy(bf16[128,32,500]{2,1,0:T(8,128)(2,1)} %reshape.126) | data formatting | bytes 8192000 | tf_op jit(solution)/shard_map/all_to_all | solution.py:48
  133.6 11.5 %all-to-all-start = ((bf16[128,32,500]{0,2,1:T(8,128)(2,1)}), bf16[128,32,500]{0,2,1:T(8,128)(2,1)}, u32[]{:S(2)}, u32[]{:S(2)}) async-start(bf16[128,32,500]{0,2,1:T(8,128)(2,1)} %copy.40), calls=%async_computation | async-start | bytes 8257536 | tf_op jit(solution)/shard_map/all_to_all | solution.py:48
  146.8 146.2 %all-reduce = s32[640]{0:T(1024)S(1)} all-reduce(s32[640]{0:T(1024)S(1)} %select_dynamic-update-slice_fusion), channel_id=1, replica_groups=mesh['dp'=32,'vocab'=8] {'dp'}, use_global_device_ids=true, to_apply=%add | all-reduce | flops 640 | bytes 5120
  293.0 3.8 reshape.123
  296.8 4.1 fusion.8
  301.0 6.6 copy.38
  307.5 18.4 %all-gather.4.cloned.1.call-done = bf16[4096,2304]{1,0:T(8,128)(2,1)} async-done(((bf16[128,2304]{1,0:T(8,128)(2,1)}), bf16[4096,2304]{1,0:T(8,128)(2,1)}) %all-gather.4.cloned.1.call-update) | async-done | bytes 18874384 | tf_op jit(solution)/shard_map/all_gather | solution.py:52
  326.0 18.5 %fusion.4 = (f32[2304]{0:T(1024)S(1)}, f32[500]{0:T(512)S(1)}, f32[500,2304]{1,0:T(8,128)}) fusion(f32[500,2304]{1,0:T(8,128)} %fusion.8, bf16[4096,500]{1,0:T(8,128)(2,1)} %bitcast.14, bf16[4096,2304]{1,0:T(8,128)(2,1)} %all-gather.4.cloned.1.call-done), kind=kOutput, calls=%fused_computation.12 | convolution fusion | flops 9442941952 | bytes 32197584 | tf_op jit(solution)/shard_map/tv,td->vd/dot_general | solution.py:49
  345.1 129.5 %all-reduce.3 = (f32[]{:T(128)}, f32[2304]{0:T(1024)S(1)}) all-reduce(f32[]{:T(128)} %get-tuple-element.10, f32[2304]{0:T(1024)S(1)} %get-tuple-element.4), channel_id=1, replica_groups=mesh['dp'=32,'vocab'=8] {'dp'}, use_global_device_ids=true, to_apply=%region_15.16 | all-reduce | flops 2305 | bytes 18440 | tf_op jit(solution)/shard_map/psum | solution.py:79
  474.6 24.6 %all-reduce.4 = (f32[]{:T(128)}, f32[2304]{0:T(1024)S(1)}) all-reduce(f32[]{:T(128)} %get-tuple-element.6, f32[2304]{0:T(1024)S(1)} %get-tuple-element.7), channel_id=1, replica_groups=mesh['dp'=32,'vocab'=8] {'vocab'}, use_global_device_ids=true, to_apply=%region_16.17 | all-reduce | flops 2305 | bytes 18440 | tf_op jit(solution)/shard_map/psum | solution.py:78
  499.9 5.8 convolution_convert_fusion
  505.7 88.9 %fusion = bf16[24,2304]{1,0:T(8,128)(2,1)S(1)} fusion(bf16[640,2304]{1,0:T(8,128)(2,1)S(1)} %convolution_convert_fusion), kind=kCustom, calls=%all-reduce-scatter | all-reduce-scatter fusion | flops 1769473 | bytes 3060736
  594.6 1.9 collective-permute-start.5
  596.5 1.9 collective-permute-start
  598.5 1.9 collective-permute-start.1
  600.4 1.9 collective-permute-start.2
  602.3 8.5 %collective-permute-start.3 = (bf16[24,2304]{1,0:T(8,128)(2,1)S(1)}, bf16[24,2304]{1,0:T(8,128)(2,1)S(1)}, u32[]{:S(2)}, u32[]{:S(2)}) collective-permute-start(bf16[24,2304]{1,0:T(8,128)(2,1)S(1)} %fusion), channel_id=1, source_target_pairs={{0,32},{8,40},{16,48},{24,56},{32,64},{40,72},{48,80},{56,88},{64,... | collective-permute-start | bytes 331784
  610.8 11.6 %collective-permute-start.4 = (bf16[24,2304]{1,0:T(8,128)(2,1)S(1)}, bf16[24,2304]{1,0:T(8,128)(2,1)S(1)}, u32[]{:S(2)}, u32[]{:S(2)}) collective-permute-start(bf16[24,2304]{1,0:T(8,128)(2,1)S(1)} %fusion), channel_id=1, source_target_pairs={{0,40},{8,48},{16,56},{24,64},{32,72},{40,80},{48,88},{56,96},{64,... | collective-permute-start | bytes 331784
  624.7 2.1 concatenate.4
  626.8 1.9 convolution_convert_fusion.1
  628.7 4.5 fusion.23
  633.2 64.1 %all-reduce.7.cloned.1.call-done = bf16[128,2304]{1,0:T(8,128)(2,1)} async-done(((bf16[128,2304]{1,0:T(8,128)(2,1)}), bf16[128,2304]{1,0:T(8,128)(2,1)}) %all-reduce.7.cloned.1.call-update) | async-done | bytes 589840 | tf_op jit(solution)/shard_map/psum | solution.py:95
  697.3 1.9 copy.43
  (79 shorter events, 8.1 us)
Async XLA Ops:
  7.2 1.2 copy-start
  7.2 3.8 copy-start.2
  7.2 285.8 %all-gather.6.cloned.1.call-start = ((), (), s32[]{:S(2)}) async-start(), calls=%async_computation.3 | async-start | bytes 3649536 | tf_op jit(solution)/shard_map/all_gather | solution.py:70
  8.0 138.6 %copy-start.9 = (pred[128]{0:T(512)(128)(4,1)}, pred[128]{0:T(512)(128)(4,1)S(1)}, u32[]{:S(2)}) copy-start(pred[128]{0:T(512)(128)(4,1)S(1)} %get-tuple-element.13) | copy-start | bytes 388
  8.4 138.2 %copy-start.8 = (s32[128]{0:T(128)}, s32[128]{0:T(128)S(1)}, u32[]{:S(2)}) copy-start(s32[128]{0:T(128)S(1)} %add_reduce_fusion) | copy-start | bytes 1540
  9.3 316.7 %all-gather.4.cloned.1.call-start = ((), (), s32[]{:S(2)}) async-start(), calls=%async_computation.1 | async-start | bytes 19464192 | tf_op jit(solution)/shard_map/all_gather | solution.py:52
  11.0 23.3 %copy-start.14 = (s32[2]{0:T(128)S(1)}, s32[2]{0:T(128)}, u32[]{:S(2)}) copy-start(s32[2]{0:T(128)} %constant.64) | copy-start | bytes 28
  11.0 23.3 %copy-start.13 = (s32[2]{0:T(128)S(1)}, s32[2]{0:T(128)}, u32[]{:S(2)}) copy-start(s32[2]{0:T(128)} %constant.67) | copy-start | bytes 28
  11.0 23.7 %copy-start.4 = (f32[128,32]{0,1:T(8,128)S(1)}, f32[128,32]{0,1:T(8,128)}, u32[]{:S(2)}) copy-start(f32[128,32]{0,1:T(8,128)} %param.15) | copy-start | bytes 49156
  133.6 11.6 %copy-start.12 = (u32[256]{0:T(256)S(1)}, u32[256]{0:T(256)}, u32[]{:S(2)}) copy-start(u32[256]{0:T(256)} %constant.74) | copy-start | bytes 3076
  133.6 13.0 %copy-start.11 = (s32[128]{0:T(128)S(1)}, s32[128]{0:T(128)}, u32[]{:S(2)}) copy-start(s32[128]{0:T(128)} %param.13) | copy-start | bytes 1540
  133.6 167.3 %all-to-all-start = ((bf16[128,32,500]{0,2,1:T(8,128)(2,1)}), bf16[128,32,500]{0,2,1:T(8,128)(2,1)}, u32[]{:S(2)}, u32[]{:S(2)}) async-start(bf16[128,32,500]{0,2,1:T(8,128)(2,1)} %copy.40), calls=%async_computation | async-start | bytes 8257536 | tf_op jit(solution)/shard_map/all_to_all | solution.py:48
  145.2 552.1 %all-reduce.7.cloned.1.call-start = ((), (), s32[]{:S(2)}) async-start(), calls=%async_computation.2 | async-start | bytes 1179648 | tf_op jit(solution)/shard_map/psum | solution.py:95
  326.0 18.5 %copy-start.10 = (f32[500]{0:T(512)S(1)}, f32[500]{0:T(512)}, u32[]{:S(2)}) copy-start(f32[500]{0:T(512)} %param.18) | copy-start | bytes 6004
  326.0 173.2 %copy-start.6 = (f32[2304]{0:T(1024)S(1)}, f32[2304]{0:T(1024)}, u32[]{:S(2)}) copy-start(f32[2304]{0:T(1024)} %param.19) | copy-start | bytes 27652
  345.1 283.6 %copy-start.7 = (f32[500]{0:T(512)}, f32[500]{0:T(512)S(1)}, u32[]{:S(2)}) copy-start(f32[500]{0:T(512)S(1)} %get-tuple-element.18) | copy-start | bytes 6004
  499.2 129.5 %copy-start.5 = (f32[2304]{0:T(1024)}, f32[2304]{0:T(1024)S(1)}, u32[]{:S(2)}) copy-start(f32[2304]{0:T(1024)S(1)} %multiply_add_fusion.1) | copy-start | bytes 27652
  594.6 28.5 %copy-start.3 = (bf16[24,2304]{1,0:T(8,128)(2,1)}, bf16[24,2304]{1,0:T(8,128)(2,1)S(1)}, u32[]{:S(2)}) copy-start(bf16[24,2304]{1,0:T(8,128)(2,1)S(1)} %fusion) | copy-start | bytes 331780
  594.6 16.2 %collective-permute-start.5 = (bf16[4,2304]{1,0:T(4,128)(2,1)S(1)}, bf16[4,2304]{1,0:T(4,128)(2,1)S(1)}, u32[]{:S(2)}, u32[]{:S(2)}) collective-permute-start(bf16[4,2304]{1,0:T(4,128)(2,1)S(1)} %slice.2), channel_id=1, source_target_pairs={{0,48},{8,56},{16,64},{24,72},{32,80},{40,88},{48,96},{56,104},{64... | collective-permute-start | bytes 55304
  596.5 26.5 %collective-permute-start = (bf16[24,2304]{1,0:T(8,128)(2,1)S(1)}, bf16[24,2304]{1,0:T(8,128)(2,1)S(1)}, u32[]{:S(2)}, u32[]{:S(2)}) collective-permute-start(bf16[24,2304]{1,0:T(8,128)(2,1)S(1)} %fusion), channel_id=1, source_target_pairs={{0,8},{8,16},{16,24},{24,32},{32,40},{40,48},{48,56},{56,64},{64,7... | collective-permute-start | bytes 331784
  598.5 24.6 %collective-permute-start.1 = (bf16[24,2304]{1,0:T(8,128)(2,1)S(1)}, bf16[24,2304]{1,0:T(8,128)(2,1)S(1)}, u32[]{:S(2)}, u32[]{:S(2)}) collective-permute-start(bf16[24,2304]{1,0:T(8,128)(2,1)S(1)} %fusion), channel_id=1, source_target_pairs={{0,16},{8,24},{16,32},{24,40},{32,48},{40,56},{48,64},{56,72},{64,... | collective-permute-start | bytes 331784
  600.4 22.7 %collective-permute-start.2 = (bf16[24,2304]{1,0:T(8,128)(2,1)S(1)}, bf16[24,2304]{1,0:T(8,128)(2,1)S(1)}, u32[]{:S(2)}, u32[]{:S(2)}) collective-permute-start(bf16[24,2304]{1,0:T(8,128)(2,1)S(1)} %fusion), channel_id=1, source_target_pairs={{0,24},{8,32},{16,40},{24,48},{32,56},{40,64},{48,72},{56,80},{64,... | collective-permute-start | bytes 331784
  602.3 20.8 %collective-permute-start.3 = (bf16[24,2304]{1,0:T(8,128)(2,1)S(1)}, bf16[24,2304]{1,0:T(8,128)(2,1)S(1)}, u32[]{:S(2)}, u32[]{:S(2)}) collective-permute-start(bf16[24,2304]{1,0:T(8,128)(2,1)S(1)} %fusion), channel_id=1, source_target_pairs={{0,32},{8,40},{16,48},{24,56},{32,64},{40,72},{48,80},{56,88},{64,... | collective-permute-start | bytes 331784
  610.8 13.9 %collective-permute-start.4 = (bf16[24,2304]{1,0:T(8,128)(2,1)S(1)}, bf16[24,2304]{1,0:T(8,128)(2,1)S(1)}, u32[]{:S(2)}, u32[]{:S(2)}) collective-permute-start(bf16[24,2304]{1,0:T(8,128)(2,1)S(1)} %fusion), channel_id=1, source_target_pairs={{0,40},{8,48},{16,56},{24,64},{32,72},{40,80},{48,88},{56,96},{64,... | collective-permute-start | bytes 331784
  624.7 74.5 %copy-start.1 = (bf16[128,2304]{1,0:T(8,128)(2,1)S(1)}, bf16[128,2304]{1,0:T(8,128)(2,1)}, u32[]{:S(2)}) copy-start(bf16[128,2304]{1,0:T(8,128)(2,1)} %param.12) | copy-start | bytes 1769476
Sparse Core Ops, SparseCore 0:
  11.2 81.9 all-gather.5
  95.7 230.1 all-gather.3
  628.8 68.4 all-reduce.6
